TPU v7x, 256 devices: a whole 4x4x8 slice. The times are simulated.
256 devices in a mesh: lat: 32 (over z_hi, y, core), chan: 8 (over z_lo, x).
Axes of the slice: x: 4, y: 4, z: 8 (z_hi: 4, z_lo: 2; z = z_hi * 2 + z_lo), core: 2. Of those that a mesh axis runs over, the one named last changes fastest.
Arguments:
- fields: float32 [256, 900, 768], P(('lat', 'chan')), may hold values from -6 to 6
- first_gain: float32 [768], replicated, may hold values from 0.5 to 1.5
- first_shift: float32 [768], replicated, may hold values from -1.5 to 1.5
- filter_one: float32 [8, 2, 96, 96], P('chan'), may hold values from -0.4375 to 0.4375
- filter_one_bias: float32 [8, 2, 96], P('chan'), may hold values from -2.5 to 2.5
- filter_two: float32 [8, 2, 96, 96], P('chan'), may hold values from -0.4375 to 0.4375
- filter_two_bias: float32 [8, 2, 96], P('chan'), may hold values from -2.5 to 2.5
- second_gain: float32 [768], replicated, may hold values from 0.5 to 1.5
- second_shift: float32 [768], replicated, may hold values from -1.5 to 1.5
- dense_weights: bfloat16 [3072, 2, 768], P(('lat', 'chan')), may hold values from -0.21875 to 0.21875
- dense_bias: bfloat16 [3072], P(('lat', 'chan')), may hold values from -2.5 to 2.5
- output_bias: float32 [768], replicated, may hold values from -1.5 to 1.5
Outputs:
- block_output: float32 [256, 900, 768], P(('lat', 'chan'))
All inputs are finite; a program needn't handle non-finite values.
Results may differ from a plain program's by a relative error of at most 0.0025.
Values may be sent and summed in bfloat16 or wider, within the bound.
No kernel may reach another device: no remote copies, remote signals or barrier semaphores. Data moves between devices by JAX's collectives and lax.ppermute only.
A program may use at most 128 MiB of HBM per device.

v0:
```python
import jax
import jax.numpy as jnp
from jax import lax
from jax.sharding import PartitionSpec as P

KW = 256
exact_mode = lax.Precision.HIGHEST
norm_eps = 1e-05
shrink_level = 0.01
two_pi = 6.283185307179586


def layer_norm(values, gain_terms, shift_terms):
    mean_value = jnp.mean(values, axis=-1, keepdims=True)
    centered = values - mean_value
    variance = jnp.mean(centered * centered, axis=-1, keepdims=True)
    return centered * lax.rsqrt(variance + norm_eps) * gain_terms + shift_terms


def soft_shrink(values):
    return jnp.sign(values) * jnp.maximum(jnp.abs(values) - shrink_level, 0.0)


def mixing_matrix(weight):
    real_weight = weight[:, 0]
    imag_weight = weight[:, 1]
    return jnp.stack(
        [jnp.stack([real_weight, imag_weight]), jnp.stack([-imag_weight, real_weight])]
    )


def complex_layer(spectrum, weight, bias_terms):
    product = jnp.einsum(
        "hakni,abnio->hbkno", spectrum, mixing_matrix(weight), precision=exact_mode
    )
    return product + jnp.transpose(bias_terms, (1, 0, 2))[None, :, None]


def per_device(
    fields,
    first_gain,
    first_shift,
    filter_one,
    filter_one_bias,
    filter_two,
    filter_two_bias,
    second_gain,
    second_shift,
    dense_weights,
    dense_bias,
    output_bias,
):
    row_count, width_count, channels = fields.shape
    lat_count = lax.axis_size("lat")
    chan_count = lax.axis_size("chan")
    height = row_count * lat_count * chan_count
    block_size = filter_one.shape[-1]
    local_blocks = filter_one.shape[0]
    local_modes = KW // lat_count
    normed_in = layer_norm(fields, first_gain, first_shift)
    lon_index = jnp.arange(width_count, dtype=jnp.int32)
    mode_index = jnp.arange(KW, dtype=jnp.int32)
    lon_angle = (
        two_pi
        / width_count
        * (lon_index[:, None] * mode_index[None, :] % width_count).astype(jnp.float32)
    )
    forward_lon = jnp.stack([jnp.cos(lon_angle), -jnp.sin(lon_angle)], axis=1) * width_count ** (
        -0.5
    )
    lon_modes = jnp.einsum("rwc,wak->rakc", normed_in, forward_lon, precision=exact_mode)
    moved = lax.all_to_all(
        lax.all_to_all(lon_modes, "lat", split_axis=2, concat_axis=0, tiled=True),
        "chan",
        split_axis=3,
        concat_axis=0,
        tiled=True,
    )
    position = jnp.arange(height, dtype=jnp.int32)
    true_row = (
        position // row_count % lat_count * chan_count + position // (row_count * lat_count)
    ) * row_count + position % row_count
    lat_index = jnp.arange(height, dtype=jnp.int32)
    forward_angle = (
        two_pi / height * (true_row[:, None] * lat_index[None, :] % height).astype(jnp.float32)
    )
    cos_forward = jnp.cos(forward_angle)
    sin_forward = jnp.sin(forward_angle)
    forward_lat = jnp.stack(
        [
            jnp.stack([cos_forward, -sin_forward], axis=1),
            jnp.stack([sin_forward, cos_forward], axis=1),
        ],
        axis=1,
    ) * height ** (-0.5)
    flat_moved = moved.reshape(height, 2, local_modes * moved.shape[3])
    spectrum = jnp.einsum("pax,pabm->mbx", flat_moved, forward_lat, precision=exact_mode)
    spectrum = spectrum.reshape(height, 2, local_modes, local_blocks, block_size)
    first_out = jnp.maximum(complex_layer(spectrum, filter_one, filter_one_bias), 0.0)
    second_out = soft_shrink(complex_layer(first_out, filter_two, filter_two_bias))
    back_angle = (
        two_pi / height * (lat_index[:, None] * lat_index[None, :] % height).astype(jnp.float32)
    )
    cos_back = jnp.cos(back_angle)
    sin_back = jnp.sin(back_angle)
    inverse_lat = jnp.stack(
        [jnp.stack([cos_back, sin_back], axis=1), jnp.stack([-sin_back, cos_back], axis=1)], axis=1
    ) * height ** (-0.5)
    lat_back = jnp.einsum(
        "max,mabh->hbx", second_out.reshape(height, 2, -1), inverse_lat, precision=exact_mode
    )
    lat_back = lat_back.reshape(height, 2, local_modes, -1)
    returned = lax.all_to_all(
        lax.all_to_all(lat_back, "lat", split_axis=0, concat_axis=2, tiled=True),
        "chan",
        split_axis=0,
        concat_axis=3,
        tiled=True,
    )
    mode_factor = jnp.where(mode_index == 0, 1.0, 2.0).astype(jnp.float32) * width_count ** (-0.5)
    inverse_lon = jnp.stack(
        [jnp.cos(lon_angle).T * mode_factor[:, None], -jnp.sin(lon_angle).T * mode_factor[:, None]]
    )
    filtered = jnp.einsum("rakc,akw->rwc", returned, inverse_lon, precision=exact_mode) + normed_in
    summed = filtered + fields
    token_count = row_count * width_count
    flat_normed = (
        layer_norm(summed, second_gain, second_shift)
        .astype(jnp.bfloat16)
        .reshape(token_count, channels)
    )
    weight_block = lax.all_gather(dense_weights, ("lat", "chan"), axis=0, tiled=True)
    bias_block = lax.all_gather(dense_bias, ("lat", "chan"), axis=0, tiled=True)
    pre_act = lax.dot_general(
        flat_normed,
        weight_block[:, 0, :],
        (((1,), (1,)), ((), ())),
        preferred_element_type=jnp.float32,
    ) + bias_block.astype(jnp.float32)
    hidden = jax.nn.gelu(pre_act, approximate=False).astype(jnp.bfloat16)
    dense_out = jnp.dot(hidden, weight_block[:, 1, :], preferred_element_type=jnp.float32)
    return summed + (dense_out + output_bias).reshape(row_count, width_count, channels)


def solution(mesh):
    placed = (
        P(("lat", "chan"), None, None),
        P(),
        P(),
        P("chan", None, None, None),
        P("chan", None, None),
        P("chan", None, None, None),
        P("chan", None, None),
        P(),
        P(),
        P(("lat", "chan"), None, None),
        P(("lat", "chan")),
        P(),
    )
    return jax.shard_map(
        per_device,
        mesh=mesh,
        in_specs=placed,
        out_specs=P(("lat", "chan"), None, None),
        check_vma=False,
    )
```

profile of v0, /device:TPU:99, one launch (start us, length us, event | category | flops | bytes accessed | tf_op | source)
XLA Modules:
  0.0 880.4 jit_solution(15925368327343979689)
XLA Ops:
  7.3 4.7 reduce_sum.36
  12.0 3.8 sine_negate_fusion
  16.3 6.4 fusion.34
  23.9 49.0 %all_to_all.66 = f32[1,2,256,768]{3,1,0,2:T(2,128)} all-to-all(f32[1,2,256,768]{3,1,0,2:T(2,128)S(1)} %copy.106), channel_id=1, replica_groups=mesh['lat'=32,'chan'=8] {'lat'}, dimensions={2} | all-to-all | bytes 3145728 | tf_op jit(solution)/shard_map/all_to_all | solution.py:73
  72.9 6.5 copy.107
  79.4 5.9 bitcast_bitcast_fusion
  85.3 7.6 reshape.513
  93.0 6.6 all-to-all-start.1
  105.8 14.5 %all-to-all-done.1 = f32[8,1,49152]{2,1,0:T(1,128)} async-done(((f32[8,1,49152]{2,1,0:T(1,128)}), f32[8,1,49152]{2,1,0:T(1,128)}, u32[]{:S(2)}, u32[]{:S(2)}) %all-to-all-start.1) | async-done | bytes 1572896 | tf_op jit(solution)/shard_map/all_to_all | solution.py:72
  120.8 6.9 reduce.4
  127.7 6.2 reshape.514
  133.9 5.9 copy.108
  142.8 5.6 convolution_bitcast_fusion.1
  156.6 3.9 convolution_bitcast_fusion
  166.4 56.5 %all_to_all.67 = f32[256,2,8,96]{3,2,1,0:T(8,128)S(1)} all-to-all(f32[256,2,8,96]{3,2,1,0:T(8,128)} %copy.114), channel_id=1, replica_groups=mesh['lat'=32,'chan'=8] {'lat'}, dimensions={0} | all-to-all | bytes 3145728 | tf_op jit(solution)/shard_map/all_to_all | solution.py:114
  227.2 5.3 all-to-all-start.3
  232.8 84.4 %all-reduce = bf16[3072]{0:T(1024)(128)(2,1)S(1)} all-reduce(bf16[3072]{0:T(1024)(128)(2,1)S(1)} %dynamic-update-slice), channel_id=1, replica_groups=mesh['lat'=32,'chan'=8] {'lat','chan'}, use_global_device_ids=true, to_apply=%add | all-reduce | flops 3072 | bytes 12288
  317.2 4.9 cosine_multiply_fusion
  324.1 5.3 fusion.140
  331.4 480.4 %all-gather.2.cloned.1.call-done = bf16[3072,2,768]{2,1,0:T(2,128)(2,1)} async-done(((bf16[12,2,768]{2,1,0:T(2,128)(2,1)}), bf16[3072,2,768]{2,1,0:T(2,128)(2,1)}) %all-gather.2.cloned.1.call-update) | async-done | bytes 9437200 | tf_op jit(solution)/shard_map/all_gather | solution.py:132
  811.8 18.4 %fusion.137 = (bf16[3072,1,768]{2,1,0:T(2,128)(2,1)S(1)}, bf16[3072,1,768]{2,1,0:T(2,128)(2,1)S(1)}) fusion(bf16[3072,2,768]{2,1,0:T(2,128)(2,1)} %all-gather.2.cloned.1.call-done), kind=kLoop, calls=%fused_computation.181 | loop fusion | bytes 18874368 | tf_op jit(solution)/shard_map/slice | solution.py:136
  830.3 32.1 %fusion.149 = bf16[900,3072]{1,0:T(8,128)(2,1)} fusion(f32[3072]{0:T(1024)S(1)} %convert_element_type.95, bf16[3072,1,768]{2,1,0:T(2,128)(2,1)S(1)} %get-tuple-element.5, f32[1,900,768]{2,1,0:T(8,128)} %copy-done.1, f32[768]{0:T(1024)S(1)} %copy-done.14, f32[768]{0:T(1024)S(1)} %copy-done.15, f32[900]{0:T(1024)S(1)} %add_rsqrt_fusion, ...), kind=kOutput, calls=%fused_computation.3.clone.clone.clone.clone.1 | convolution fusion | flops 4432665600 | bytes 13038624 | tf_op jit(solution)/shard_map/dot_general | solution.py:134
  862.4 6.6 bitcast_add_fusion
  869.0 4.4 copy.122
  (76 shorter events, 34.6 us)
Async XLA Ops:
  6.5 9.2 %copy-start = (f32[1,900,768]{2,0,1:T(1,128)S(1)}, f32[1,900,768]{2,0,1:T(1,128)}, u32[]{:S(2)}) copy-start(f32[1,900,768]{2,0,1:T(1,128)} %param.12) | copy-start | bytes 8294404
  6.5 805.2 %all-gather.2.cloned.1.call-start = ((), (), s32[]{:S(2)}) async-start(), calls=%async_computation.4 | async-start | bytes 9474048 | tf_op jit(solution)/shard_map/all_gather | solution.py:132
  12.0 4.3 copy-start.12
  12.0 4.3 copy-start.13
  93.0 6.6 copy-start.8
  93.0 6.8 copy-start.9
  93.0 27.3 %all-to-all-start.1 = ((f32[8,1,49152]{2,1,0:T(1,128)}), f32[8,1,49152]{2,1,0:T(1,128)}, u32[]{:S(2)}, u32[]{:S(2)}) async-start(f32[8,1,49152]{2,1,0:T(1,128)} %reshape.513), calls=%async_computation.1 | async-start | bytes 3145728 | tf_op jit(solution)/shard_map/all_to_all | solution.py:72
  142.8 8.6 copy-start.10
  148.4 6.0 copy-start.11
  151.5 3.0 copy-start.6
  151.5 3.0 copy-start.7
  151.5 5.1 copy-start.3
  224.4 8.1 copy-start.17
  227.2 95.0 %all-to-all-start.3 = ((f32[8,2,256,96]{2,3,1,0:T(8,128)}), f32[8,2,256,96]{2,3,1,0:T(8,128)}, u32[]{:S(2)}, u32[]{:S(2)}) async-start(f32[8,2,256,96]{2,3,1,0:T(8,128)} %copy.116), calls=%async_computation.3 | async-start | bytes 3145728 | tf_op jit(solution)/shard_map/all_to_all | solution.py:113
  322.1 1.7 copy-start.4
  322.1 1.9 copy-start.5
  329.4 1.5 copy-start.1
  331.4 498.9 %copy-start.14 = (f32[768]{0:T(1024)S(1)}, f32[768]{0:T(1024)}, u32[]{:S(2)}) copy-start(f32[768]{0:T(1024)} %param.20) | copy-start | bytes 9220
  331.4 498.9 %copy-start.15 = (f32[768]{0:T(1024)S(1)}, f32[768]{0:T(1024)}, u32[]{:S(2)}) copy-start(f32[768]{0:T(1024)} %param.19) | copy-start | bytes 9220
  830.2 32.1 %copy-start.2 = (f32[1,900,768]{2,1,0:T(8,128)S(1)}, f32[1,900,768]{2,1,0:T(8,128)}, u32[]{:S(2)}) copy-start(f32[1,900,768]{2,1,0:T(8,128)} %copy-done.1) | copy-start | bytes 8294404
  830.2 32.1 %copy-start.16 = (f32[768]{0:T(1024)S(1)}, f32[768]{0:T(1024)}, u32[]{:S(2)}) copy-start(f32[768]{0:T(1024)} %param.23) | copy-start | bytes 9220
Sparse Core Ops, SparseCore 0:
  9.2 802.5 all-gather.1
where the time goes:
time: 890 us; the launch traced here: 880 us
  waiting for transfers between devices  496 us (56%)
  blocking collectives  190 us (21%)
  local copies, waits for them, and re-layouts  77.1 us (9%)
  matrix products  64.9 us (7%)
  other arithmetic  27 us (3%)
  between operations  14 us (2%)
  starting transfers between devices  11.9 us (1%)
    all_gather x1, waiting for transfers between devices, per_device(): lax.all_gather(dense_weights, ('lat', 'chan'), axis=0, tiled=True)  480 us
    unnamed x1, blocking collectives  84.4 us
    all_to_all x1, blocking collectives, per_device(): lax.all_to_all(lat_back, 'lat', split_axis=0, concat_axis=2, tiled=True)  56.5 us
    all_to_all x1, blocking collectives, per_device(): lax.all_to_all(lon_modes, 'lat', split_axis=2, concat_axis=0, tiled=True)  49 us
    dot_general x1, matrix products, per_device(): lax.dot_general(flat_normed, weight_block[:, 0, :], (((1,), (1,)), ((), (...  32.1 us
    unnamed x45, local copies, waits for them, and re-layouts  22.1 us
    slice x1, local copies, waits for them, and re-layouts, per_device(): weight_block[:, 0, :]  18.4 us
  transfers between devices with their start and end apart: 3, of which 2 were waited for; matrix products, arithmetic and copies ran while one was open for 12% of the time, Pallas kernels for 0%

commit v1 on v0

--- a/solution.py
+++ b/solution.py
@@ -129,7 +129,12 @@
         .astype(jnp.bfloat16)
         .reshape(token_count, channels)
     )
-    weight_block = lax.all_gather(dense_weights, ("lat", "chan"), axis=0, tiled=True)
+    weight_block = jnp.concatenate(
+        lax.all_to_all(
+            jnp.stack([dense_weights] * lax.axis_size(("lat", "chan"))), ("lat", "chan"), 0, 0
+        ),
+        axis=0,
+    )
     bias_block = lax.all_gather(dense_bias, ("lat", "chan"), axis=0, tiled=True)
     pre_act = lax.dot_general(
         flat_normed,

time: 890 us -> 595 us (0.67)
  the two profiles are of different devices: /device:TPU:99 before, /device:TPU:1 now
where the time goes in v1:
time: 595 us; the launch traced here: 586 us
  blocking collectives  382 us (64%)
  local copies, waits for them, and re-layouts  82.6 us (14%)
  matrix products  64.2 us (11%)
  other arithmetic  26.8 us (5%)
  waiting for transfers between devices  14.5 us (2%)
  starting transfers between devices  14.3 us (2%)
    unnamed x1, blocking collectives  249 us
    all_to_all x1, blocking collectives, per_device(): lax.all_to_all(lon_modes, 'lat', split_axis=2, concat_axis=0, tiled=True)  52.8 us
    all_to_all x1, blocking collectives, per_device(): lax.all_to_all(lat_back, 'lat', split_axis=0, concat_axis=2, tiled=True)  46.3 us
    all_to_all x1, blocking collectives, per_device(): lax.all_to_all(lax.all_to_all(lat_back, 'lat', split_axis=0, concat_axis=...  33.8 us
    dot_general x1, matrix products, per_device(): lax.dot_general(flat_normed, weight_block[:, 0, :], (((1,), (1,)), ((), (...  31.9 us
    unnamed x49, local copies, waits for them, and re-layouts  22.8 us
    slice x1, local copies, waits for them, and re-layouts, per_device(): weight_block[:, 0, :]  18.4 us
    all_to_all x1, waiting for transfers between devices, per_device(): lax.all_to_all(lax.all_to_all(lon_modes, 'lat', split_axis=2, concat_axis...  14.5 us
  transfers between devices with their start and end apart: 2, of which 1 were waited for; matrix products, arithmetic and copies ran while one was open for 3% of the time, Pallas kernels for 0%

profile of v1, /device:TPU:1, one launch (start us, length us, event | category | flops | bytes accessed | tf_op | source)
XLA Modules:
  0.0 585.7 jit_solution(6098489927003370731)
XLA Ops:
  0.0 4.8 sine_negate_fusion
  4.8 4.6 reduce_sum.36
  10.9 5.9 %fusion.44 = f32[1,2,256,768]{3,2,1,0:T(8,128)S(1)} fusion(f32[1,900,768]{2,0,1:T(1,128)S(1)} %copy-done, f32[900,1,256]{2,0,1:T(8,128)S(1)} %copy-done.5, f32[900,1,256]{2,0,1:T(8,128)S(1)} %copy-done.6, f32[768]{0:T(1024)S(1)} %copy-done.14, f32[768]{0:T(1024)S(1)} %copy-done.15, f32[900]{0:T(1024)S(1)} %add_rsqrt_fusion.1, ...), kind=kOutput, calls=%fused_computation.54 | convolution fusion | flops 4250419200 | bytes 6194208 | tf_op jit(solution)/shard_map/rwc,wak->rakc/dot_general | solution.py:71
  18.0 52.8 %all_to_all.71 = f32[1,2,256,768]{3,1,0,2:T(2,128)} all-to-all(f32[1,2,256,768]{3,1,0,2:T(2,128)S(1)} %copy.103), channel_id=1, replica_groups=mesh['lat'=32,'chan'=8] {'lat'}, dimensions={2} | all-to-all | bytes 3145728 | tf_op jit(solution)/shard_map/all_to_all | solution.py:73
  70.8 6.5 %copy.104 = f32[1,2,32,8,768]{2,3,1,4,0:T(8,128)} copy(f32[1,2,32,8,768]{4,1,3,2,0:T(2,128)} %bitcast.157) | data formatting | bytes 3145728 | tf_op jit(solution)/shard_map/all_to_all | solution.py:73
  77.3 5.8 bitcast_bitcast_fusion
  83.2 7.6 %reshape.519 = f32[8,1,49152]{2,1,0:T(1,128)} reshape(f32[768,2,8,32]{3,2,1,0:T(8,128)} %bitcast_bitcast_fusion) | data formatting | bytes 3145728
  90.8 5.0 all-to-all-start.1
  102.0 14.5 %all-to-all-done.1 = f32[8,1,49152]{2,1,0:T(1,128)} async-done(((f32[8,1,49152]{2,1,0:T(1,128)}), f32[8,1,49152]{2,1,0:T(1,128)}, u32[]{:S(2)}, u32[]{:S(2)}) %all-to-all-start.1) | async-done | bytes 1572896 | tf_op jit(solution)/shard_map/all_to_all | solution.py:72
  117.1 6.9 %reduce.4 = f32[8,49152]{1,0:T(8,128)} reduce(f32[8,1,49152]{2,1,0:T(1,128)} %all-to-all-done.1, f32[]{:T(128)} %broadcast.665), dimensions={1}, to_apply=%all_to_all.55.reduce_sub_computation | reduce | bytes 3145732 | tf_op jit(solution)/shard_map/all_to_all | solution.py:72
  124.0 6.1 %reshape.520 = f32[768,2,8,32]{3,2,1,0:T(8,128)} reshape(f32[8,49152]{1,0:T(8,128)} %reduce.4) | data formatting | bytes 3145728
  130.1 5.9 %copy.105 = f32[32,2,8,8,96]{4,2,0,3,1:T(8,128)} copy(f32[32,2,8,8,96]{0,2,1,4,3:T(8,128)} %bitcast.150) | data formatting | bytes 3145728 | tf_op jit(solution)/shard_map/all_to_all | solution.py:72
  139.3 5.6 convolution_bitcast_fusion.1
  153.1 3.9 convolution_bitcast_fusion
  162.9 46.3 %all_to_all.72 = f32[256,2,8,96]{3,2,1,0:T(8,128)S(1)} all-to-all(f32[256,2,8,96]{3,2,1,0:T(8,128)} %copy.111), channel_id=1, replica_groups=mesh['lat'=32,'chan'=8] {'lat'}, dimensions={0} | all-to-all | bytes 3145728 | tf_op jit(solution)/shard_map/all_to_all | solution.py:114
  213.6 33.8 %all_to_all.73 = f32[8,2,256,96]{2,3,1,0:T(8,128)} all-to-all(f32[8,2,256,96]{2,3,1,0:T(8,128)} %copy.113), channel_id=1, replica_groups=mesh['lat'=32,'chan'=8] {'chan'}, dimensions={0} | all-to-all | bytes 3145728 | tf_op jit(solution)/shard_map/all_to_all | solution.py:113
  247.3 6.2 %stack.68 = bf16[256,12,2,768]{3,2,1,0:T(2,128)(2,1)} broadcast(bf16[12,2,768]{2,1,0:T(2,128)(2,1)S(1)} %copy-done.11), dimensions={1,2,3} | broadcast | bytes 9474048 | tf_op jit(solution)/shard_map/stack | solution.py:134
  253.5 9.3 %all-to-all-start.4 = ((bf16[256,12,2,768]{3,2,1,0:T(2,128)(2,1)}), bf16[256,12,2,768]{3,2,1,0:T(2,128)(2,1)}, u32[]{:S(2)}, u32[]{:S(2)}) async-start(bf16[256,12,2,768]{3,2,1,0:T(2,128)(2,1)} %stack.68), calls=%async_computation.4 | async-start | bytes 18874368 | tf_op jit(solution)/shard_map/all_to_all | solution.py:133
  263.1 249.4 %all-reduce = bf16[3072]{0:T(1024)(128)(2,1)S(1)} all-reduce(bf16[3072]{0:T(1024)(128)(2,1)S(1)} %dynamic-update-slice), channel_id=1, replica_groups=mesh['lat'=32,'chan'=8] {'lat','chan'}, use_global_device_ids=true, to_apply=%add | all-reduce | flops 3072 | bytes 12288
  516.5 5.3 fusion.150
  523.9 18.4 %fusion.147 = (bf16[3072,1,768]{2,1,0:T(2,128)(2,1)S(1)}, bf16[3072,1,768]{2,1,0:T(2,128)(2,1)S(1)}) fusion(bf16[3072,2,768]{2,1,0:T(2,128)(2,1)} %bitcast.57), kind=kLoop, calls=%fused_computation.183 | loop fusion | bytes 18874368 | tf_op jit(solution)/shard_map/slice | solution.py:141
  542.3 31.9 %fusion.163 = bf16[900,3072]{1,0:T(8,128)(2,1)} fusion(f32[3072]{0:T(1024)S(1)} %convert_element_type.95, bf16[3072,1,768]{2,1,0:T(2,128)(2,1)S(1)} %get-tuple-element.5, f32[1,900,768]{2,1,0:T(8,128)} %copy-done.2, f32[768]{0:T(1024)S(1)} %copy-done.16, f32[768]{0:T(1024)S(1)} %copy-done.17, f32[900]{0:T(1024)S(1)} %add_rsqrt_fusion, ...), kind=kOutput, calls=%fused_computation.3.clone.clone.clone.clone.1 | convolution fusion | flops 4432665600 | bytes 13038624 | tf_op jit(solution)/shard_map/dot_general | solution.py:139
  574.2 6.6 %bitcast_add_fusion = f32[1,900,768]{2,1,0:T(8,128)S(1)} fusion(f32[1,900,768]{2,1,0:T(8,128)S(1)} %copy-done.3, bf16[3072,1,768]{2,1,0:T(2,128)(2,1)S(1)} %get-tuple-element.6, f32[768]{0:T(1024)S(1)} %copy-done.18, bf16[900,3072]{1,0:T(8,128)(2,1)} %fusion.163), kind=kOutput, calls=%fused_computation.25 | convolution fusion | flops 4248115200 | bytes 15780864 | tf_op jit(solution)/shard_map/dot_general | solution.py:146
  580.9 4.4 copy.117
  (79 shorter events, 37.2 us)
Async XLA Ops:
  0.0 9.4 %copy-start = (f32[1,900,768]{2,0,1:T(1,128)S(1)}, f32[1,900,768]{2,0,1:T(1,128)}, u32[]{:S(2)}) copy-start(f32[1,900,768]{2,0,1:T(1,128)} %param.12) | copy-start | bytes 8294404
  4.8 5.1 copy-start.14
  4.8 5.1 copy-start.15
  9.4 1.2 copy-start.5
  9.4 1.5 copy-start.6
  90.8 5.0 copy-start.9
  90.8 5.2 copy-start.10
  90.8 25.7 %all-to-all-start.1 = ((f32[8,1,49152]{2,1,0:T(1,128)}), f32[8,1,49152]{2,1,0:T(1,128)}, u32[]{:S(2)}, u32[]{:S(2)}) async-start(f32[8,1,49152]{2,1,0:T(1,128)} %reshape.519), calls=%async_computation.1 | async-start | bytes 3145728 | tf_op jit(solution)/shard_map/all_to_all | solution.py:72
  139.3 8.7 %copy-start.12 = (f32[1,2,96]{2,1,0:T(2,128)S(1)}, f32[1,2,96]{2,1,0:T(2,128)}, u32[]{:S(2)}) copy-start(f32[1,2,96]{2,1,0:T(2,128)} %param.16) | copy-start | bytes 2308
  144.9 6.1 %copy-start.13 = (f32[1,2,96]{2,1,0:T(2,128)S(1)}, f32[1,2,96]{2,1,0:T(2,128)}, u32[]{:S(2)}) copy-start(f32[1,2,96]{2,1,0:T(2,128)} %param.18) | copy-start | bytes 2308
  148.0 3.0 copy-start.7
  148.0 3.0 copy-start.8
  148.0 5.1 copy-start.4
  210.7 36.6 %copy-start.11 = (bf16[12,2,768]{2,1,0:T(2,128)(2,1)S(1)}, bf16[12,2,768]{2,1,0:T(2,128)(2,1)}, u32[]{:S(2)}) copy-start(bf16[12,2,768]{2,1,0:T(2,128)(2,1)} %param.21) | copy-start | bytes 110596
  253.5 9.4 %copy-start.19 = (bf16[12]{0:T(256)(128)(2,1)S(1)}, bf16[12]{0:T(256)(128)(2,1)}, u32[]{:S(2)}) copy-start(bf16[12]{0:T(256)(128)(2,1)} %param.22) | copy-start | bytes 76
  253.5 270.3 %all-to-all-start.4 = ((bf16[256,12,2,768]{3,2,1,0:T(2,128)(2,1)}), bf16[256,12,2,768]{3,2,1,0:T(2,128)(2,1)}, u32[]{:S(2)}, u32[]{:S(2)}) async-start(bf16[256,12,2,768]{3,2,1,0:T(2,128)(2,1)} %stack.68), calls=%async_computation.4 | async-start | bytes 18874368 | tf_op jit(solution)/shard_map/all_to_all | solution.py:133
  512.5 3.8 copy-start.1
  521.8 1.6 copy-start.2
  523.8 18.4 %copy-start.16 = (f32[768]{0:T(1024)S(1)}, f32[768]{0:T(1024)}, u32[]{:S(2)}) copy-start(f32[768]{0:T(1024)} %param.20) | copy-start | bytes 9220
  523.8 18.4 %copy-start.17 = (f32[768]{0:T(1024)S(1)}, f32[768]{0:T(1024)}, u32[]{:S(2)}) copy-start(f32[768]{0:T(1024)} %param.19) | copy-start | bytes 9220
  542.3 31.9 %copy-start.3 = (f32[1,900,768]{2,1,0:T(8,128)S(1)}, f32[1,900,768]{2,1,0:T(8,128)}, u32[]{:S(2)}) copy-start(f32[1,900,768]{2,1,0:T(8,128)} %copy-done.2) | copy-start | bytes 8294404
  542.3 31.9 %copy-start.18 = (f32[768]{0:T(1024)S(1)}, f32[768]{0:T(1024)}, u32[]{:S(2)}) copy-start(f32[768]{0:T(1024)} %param.23) | copy-start | bytes 9220
